TPU v7x, 512 devices: a whole 4x8x8 slice. The times are simulated.
512 devices in a mesh: section: 8 (over y), dp: 64 (over z, x, core).
Axes of the slice: x: 4, y: 8, z: 8, core: 2. Of those that a mesh axis runs over, the one named last changes fastest.
Arguments:
- fresh_acts: bfloat16 [3, 128, 8192], P(None, None, 'dp'), may hold values from -36 to 36
- carried: bfloat16 [8, 128, 8192], P('section', None, 'dp'), may hold values from -36 to 36
- norm_gain: float32 [8, 8192], P('section'), may hold values from 0.1 to 1.9
- w_in: bfloat16 [8, 3, 4096, 8192], P('section', None, 'dp'), may hold values from -0.0625 to 0.0625
- short_filter: float32 [8, 3, 4096, 3], P('section', None, 'dp'), may hold values from -3 to 3
- filter_taps: float32 [8, 4096, 128], P('section', 'dp'), may hold values from -0.9 to 0.9
- decay_rate: float32 [8, 4096], P('section', 'dp'), may hold values from 0.01 to 0.12
- w_out: bfloat16 [8, 4096, 8192], P('section', None, 'dp'), may hold values from -0.09375 to 0.09375
Outputs:
- section_outputs: bfloat16 [8, 3, 128, 8192], P('section', None, None, 'dp')
All inputs are finite; a program needn't handle non-finite values.
Results may differ from a plain program's by a relative error of at most 0.011.
Values may be sent and summed in bfloat16 or wider, within the bound.
A program may use at most 64 MiB of HBM per device.

v0:
```python
import jax
import jax.numpy as jnp
from jax import lax
from jax.sharding import PartitionSpec as P

EPS = 1e-06


def shifted(value, axis, steps):
    count = lax.axis_size(axis)
    pairs = [(source, (source + steps) % count) for source in range(count)]
    return lax.ppermute(value, axis, pairs)


def build_toeplitz(tap_values, decay_rate, tok_len):
    tap_count = tap_values.shape[1]
    lag_grid = jnp.arange(tok_len)[:, None] - jnp.arange(tok_len)[None, :]
    onehot = (lag_grid[:, :, None] == jnp.arange(tap_count)[None, None, :]).astype(jnp.float32)
    filter_vals = tap_values * jnp.exp(
        -decay_rate[:, None] * jnp.arange(tap_count, dtype=jnp.float32)[None, :]
    )
    return jnp.einsum("cj,tsj->cts", filter_vals, onehot, precision=lax.Precision.HIGHEST)


def mixing(u_proj, short_taps, toeplitz):
    tok_len = u_proj.shape[0]
    tap_count = short_taps.shape[2]
    padded = jnp.pad(u_proj, ((tap_count - 1, 0), (0, 0), (0, 0)))
    mixed_out = short_taps[:, :, 0] * u_proj
    for j in range(1, tap_count):
        mixed_out = (
            mixed_out
            + short_taps[:, :, j] * padded[tap_count - 1 - j : tap_count - 1 - j + tok_len]
        )
    query_part = mixed_out[:, 0]
    product = mixed_out[:, 1] * mixed_out[:, 2]
    long_conv = jnp.einsum("cts,sc->tc", toeplitz, product, precision=lax.Precision.HIGHEST)
    return (query_part * long_conv).astype(jnp.bfloat16)


def contract_rows(normed, weight_rows):
    return lax.dot_general(
        normed, weight_rows, (((1,), (1,)), ((), ())), preferred_element_type=jnp.float32
    )


def body(fresh_acts, carried, norm_gain, w_in, short_filter, filter_taps, decay_rate, w_out):
    section_idx = lax.axis_index("section")
    section_count = lax.axis_size("section")
    is_first = section_idx == 0
    tick_count = fresh_acts.shape[0]
    tok_len = fresh_acts.shape[1]
    feat_dev = fresh_acts.shape[2]
    model_width = norm_gain.shape[1]
    chan_dev = w_in.shape[2]
    gain_row = norm_gain[0]
    w_in_flat = w_in[0].reshape(3 * chan_dev, model_width)
    w_out_local = w_out[0]
    short_taps = short_filter[0]
    toeplitz = build_toeplitz(filter_taps[0], decay_rate[0], tok_len)
    own_start = lax.axis_index("dp") * feat_dev
    start_slice = jnp.where(is_first, fresh_acts[0], carried[0])
    results = []
    is_last = section_idx == section_count - 1
    full_rows = lax.all_gather(start_slice, "dp", axis=1, tiled=True)
    for k in range(tick_count):
        widened = full_rows.astype(jnp.float32)
        normed = (widened * gain_row).astype(jnp.bfloat16)
        from_proj_acc = contract_rows(normed, w_in_flat)
        from_sum_sq = jnp.sum(widened * widened, axis=1)
        from_own_slice = lax.dynamic_slice_in_dim(full_rows, own_start, feat_dev, 1)
        factor = lax.rsqrt(from_sum_sq / model_width + EPS)
        u_proj = (from_proj_acc * factor[:, None]).reshape(tok_len, 3, chan_dev)
        y_local = mixing(u_proj, short_taps, toeplitz)
        out_acc = jnp.dot(
            lax.all_gather(y_local, "dp", axis=1, tiled=True),
            w_out_local,
            preferred_element_type=jnp.float32,
        )
        produced = (from_own_slice.astype(jnp.float32) + out_acc).astype(jnp.bfloat16)
        results.append(produced)
        if k + 1 < tick_count:
            source = jnp.where(is_last, fresh_acts[k + 1], produced)
            gathered = lax.all_gather(source, "dp", axis=1, tiled=True)
            full_rows = shifted(gathered, "section", 1)
    return jnp.stack(results)[None]


def solution(mesh):
    return jax.shard_map(
        body,
        mesh=mesh,
        in_specs=(
            P(None, None, "dp"),
            P("section", None, "dp"),
            P("section", None),
            P("section", None, "dp", None),
            P("section", None, "dp", None),
            P("section", "dp", None),
            P("section", "dp"),
            P("section", None, "dp"),
        ),
        out_specs=P("section", None, None, "dp"),
        check_vma=False,
    )
```

profile of v0, /device:TPU:1, one launch (start us, length us, event | category | flops | bytes accessed | tf_op | source)
XLA Modules:
  0.0 632.6 jit_solution(17019697142126312985)
XLA Ops:
  6.5 1.5 slice_select_fusion
  9.5 8.1 %fusion = f32[64,128,128]{2,0,1:T(8,128)} fusion(s32[128,128]{1,0:T(8,128)S(1)} %iota_subtract_fusion, f32[1,64,128]{2,1,0:T(8,128)} %param.13, f32[64]{0:T(128)S(1)} %negate_bitcast_fusion), kind=kOutput, calls=%fused_computation.1 | convolution fusion | flops 1612726272 | bytes 4292864 | tf_op jit(solution)/shard_map/cj,tsj->cts/dot_general | solution.py:22
  17.6 5.4 copy.10
  23.0 72.1 %all-gather.18.cloned.1.call-done = bf16[1,128,8192]{2,1,0:T(8,128)(2,1)} async-done(((bf16[1,128,128]{2,1,0:T(8,128)(2,1)}), bf16[1,128,8192]{2,1,0:T(8,128)(2,1)}) %all-gather.18.cloned.1.call-update) | async-done | bytes 2097168 | tf_op jit(solution)/shard_map/all_gather | solution.py:65
  95.1 2.1 fusion.6
  97.2 2.7 fusion.24
  100.2 3.7 fusion.60
  104.6 81.2 %all-gather.8.cloned.1.call-done = bf16[128,4096]{0,1:T(8,128)(2,1)} async-done(((bf16[128,64]{0,1:T(8,128)(2,1)}), bf16[128,4096]{0,1:T(8,128)(2,1)}) %all-gather.8.cloned.1.call-update) | async-done | bytes 1048592 | tf_op jit(solution)/shard_map/all_gather | solution.py:76
  185.8 2.6 bitcast_select_fusion.1
  188.5 76.4 %all-gather.10.cloned.1.call-done = bf16[128,8192]{1,0:T(8,128)(2,1)} async-done(((bf16[128,128]{1,0:T(8,128)(2,1)}), bf16[128,8192]{1,0:T(8,128)(2,1)}) %all-gather.10.cloned.1.call-update) | async-done | bytes 2097168 | tf_op jit(solution)/shard_map/all_gather | solution.py:84
  264.9 3.3 collective-permute-start
  268.2 47.0 %collective-permute-done = bf16[128,8192]{1,0:T(8,128)(2,1)S(1)} collective-permute-done((bf16[128,8192]{1,0:T(8,128)(2,1)}, bf16[128,8192]{1,0:T(8,128)(2,1)S(1)}, u32[]{:S(2)}, u32[]{:S(2)}) %collective-permute-start) | collective-permute-done | bytes 2097184 | tf_op jit(solution)/shard_map/ppermute | solution.py:12
  315.7 1.1 fusion.18
  317.0 1.1 copy-done.2
  318.1 3.6 fusion.61
  322.5 82.1 %all-gather.12.cloned.1.call-done = bf16[128,4096]{0,1:T(8,128)(2,1)} async-done(((bf16[128,64]{0,1:T(8,128)(2,1)}), bf16[128,4096]{0,1:T(8,128)(2,1)}) %all-gather.12.cloned.1.call-update) | async-done | bytes 1048592 | tf_op jit(solution)/shard_map/all_gather | solution.py:76
  404.5 2.6 bitcast_select_fusion
  407.3 76.3 %all-gather.14.cloned.1.call-done = bf16[128,8192]{1,0:T(8,128)(2,1)} async-done(((bf16[128,128]{1,0:T(8,128)(2,1)}), bf16[128,8192]{1,0:T(8,128)(2,1)}) %all-gather.14.cloned.1.call-update) | async-done | bytes 2097168 | tf_op jit(solution)/shard_map/all_gather | solution.py:84
  483.5 3.1 collective-permute-start.1
  486.6 47.2 %collective-permute-done.1 = bf16[128,8192]{1,0:T(8,128)(2,1)S(1)} collective-permute-done((bf16[128,8192]{1,0:T(8,128)(2,1)}, bf16[128,8192]{1,0:T(8,128)(2,1)S(1)}, u32[]{:S(2)}, u32[]{:S(2)}) %collective-permute-start.1) | collective-permute-done | bytes 2097184 | tf_op jit(solution)/shard_map/ppermute | solution.py:12
  535.6 1.1 copy-done.3
  536.7 3.6 fusion.62
  541.0 82.1 %all-gather.16.cloned.1.call-done = bf16[128,4096]{0,1:T(8,128)(2,1)} async-done(((bf16[128,64]{0,1:T(8,128)(2,1)}), bf16[128,4096]{0,1:T(8,128)(2,1)}) %all-gather.16.cloned.1.call-update) | async-done | bytes 1048592 | tf_op jit(solution)/shard_map/all_gather | solution.py:76
  623.1 2.0 fusion.45
  (48 shorter events, 6.9 us)
Async XLA Ops:
  6.5 90.7 %copy-start = (bf16[1,3,64,8192]{3,2,1,0:T(8,128)(2,1)S(1)}, bf16[1,3,64,8192]{3,2,1,0:T(8,128)(2,1)}, u32[]{:S(2)}) copy-start(bf16[1,3,64,8192]{3,2,1,0:T(8,128)(2,1)} %param.11) | copy-start | bytes 9437188
  6.5 88.6 %all-gather.18.cloned.1.call-start = ((), (), s32[]{:S(2)}) async-start(), calls=%async_computation.5 | async-start | bytes 2129920 | tf_op jit(solution)/shard_map/all_gather | solution.py:65
  8.1 177.7 %all-gather.8.cloned.1.call-start = ((), (), s32[]{:S(2)}) async-start(), calls=%async_computation | async-start | bytes 1064960 | tf_op jit(solution)/shard_map/all_gather | solution.py:76
  17.6 79.6 %copy-start.7 = (f32[1,8192]{1,0:T(1,128)S(1)}, f32[1,8192]{1,0:T(1,128)}, u32[]{:S(2)}) copy-start(f32[1,8192]{1,0:T(1,128)} %param.10) | copy-start | bytes 98308
  97.2 3.0 copy-start.1
  100.0 85.8 %copy-start.6 = (bf16[3,128,128]{2,1,0:T(8,128)(2,1)S(1)}, bf16[3,128,128]{2,1,0:T(8,128)(2,1)}, u32[]{:S(2)}) copy-start(bf16[3,128,128]{2,1,0:T(8,128)(2,1)} %param.8) | copy-start | bytes 294916
  104.5 160.4 %all-gather.10.cloned.1.call-start = ((), (), s32[]{:S(2)}) async-start(), calls=%async_computation.1 | async-start | bytes 2129920 | tf_op jit(solution)/shard_map/all_gather | solution.py:84
  188.5 216.1 %all-gather.12.cloned.1.call-start = ((), (), s32[]{:S(2)}) async-start(), calls=%async_computation.2 | async-start | bytes 1064960 | tf_op jit(solution)/shard_map/all_gather | solution.py:76
  264.9 50.3 %collective-permute-start = (bf16[128,8192]{1,0:T(8,128)(2,1)}, bf16[128,8192]{1,0:T(8,128)(2,1)S(1)}, u32[]{:S(2)}, u32[]{:S(2)}) collective-permute-start(bf16[128,8192]{1,0:T(8,128)(2,1)} %all-gather.10.cloned.1.call-done), channel_id=1, source_target_pairs={{0,64},{64,128},{128,192},{192,256},{256,320},{320,384},{384,448},... | collective-permute-start | bytes 6291464 | tf_op jit(solution)/shard_map/ppermute | solution.py:12
  315.2 1.6 copy-start.4
  315.7 2.4 copy-start.2
  322.4 161.1 %all-gather.14.cloned.1.call-start = ((), (), s32[]{:S(2)}) async-start(), calls=%async_computation.3 | async-start | bytes 2129920 | tf_op jit(solution)/shard_map/all_gather | solution.py:84
  407.2 215.9 %all-gather.16.cloned.1.call-start = ((), (), s32[]{:S(2)}) async-start(), calls=%async_computation.4 | async-start | bytes 1064960 | tf_op jit(solution)/shard_map/all_gather | solution.py:76
  483.5 50.3 %collective-permute-start.1 = (bf16[128,8192]{1,0:T(8,128)(2,1)}, bf16[128,8192]{1,0:T(8,128)(2,1)S(1)}, u32[]{:S(2)}, u32[]{:S(2)}) collective-permute-start(bf16[128,8192]{1,0:T(8,128)(2,1)} %all-gather.14.cloned.1.call-done), channel_id=1, source_target_pairs={{0,64},{64,128},{128,192},{192,256},{256,320},{320,384},{384,448},... | collective-permute-start | bytes 6291464 | tf_op jit(solution)/shard_map/ppermute | solution.py:12
  533.8 1.6 copy-start.5
  534.3 2.4 copy-start.3
Sparse Core Ops, SparseCore 0:
  10.6 84.5 all-gather.17
  104.6 81.1 all-gather.7
  189.0 75.8 all-gather.9
  322.6 81.9 all-gather.11
  407.6 75.8 all-gather.13
  541.1 81.9 all-gather.15
where the time goes:
time: 633 us
  waiting for transfers between devices  564 us (89%)
  matrix products  31.2 us (5%)
  between operations  13.7 us (2%)
  other arithmetic  8.37 us (1%)
  local copies, waits for them, and re-layouts  8.34 us (1%)
  starting transfers between devices  6.59 us (1%)
    all_gather x3, waiting for transfers between devices, body(): lax.all_gather(y_local, 'dp', axis=1, tiled=True)  245 us
    all_gather x2, waiting for transfers between devices, body(): gathered = lax.all_gather(source, 'dp', axis=1, tiled=True)  153 us
    ppermute x2, waiting for transfers between devices, shifted(): return lax.ppermute(value, axis, pairs)  94.2 us
    all_gather x1, waiting for transfers between devices, body(): full_rows = lax.all_gather(start_slice, 'dp', axis=1, tiled=True)  72.1 us
  transfers between devices with their start and end apart: 8, of which 8 were waited for; matrix products, arithmetic and copies ran while one was open for 2% of the time, Pallas kernels for 0%

commit v1 on v0

v1 whole, which is shorter than its diff:
```python
import jax
import jax.numpy as jnp
from jax import lax
from jax.experimental import pallas as pl
from jax.experimental.pallas import tpu as pltpu
from jax.sharding import PartitionSpec as P

EPS = 1e-06
MESH = pl.DeviceIdType.MESH
F32 = jnp.float32
BF16 = jnp.bfloat16

NZ, NX, NS = 8, 4, 8
NP = NZ * NX
TICKS, SEQ, FD, CD, D = 3, 128, 128, 64, 8192
Z_ORDER = (1, 7, 2, 6, 3, 5, 4)
X_ORDER = (1, 3, 2)
GROUP = 2


def kernel(
    fresh, carried, gain, w_in, taps_hbm, long_hbm, decay_hbm, w_out, out,
    acts, gated, produced, result, w1, w2raw, w2, gain_v, fresh_v, carried_v,
    taps_v, long_v, decay_v, taps_sq, taps_row, long_row, normed, acc, acc_in, u_pad, p_pad, fin_out, fin_in,
    sem_in, sem_w, sem_wsend, sem_wrecv, a_send, a_recv, y_send, y_recv, x_send, x_recv, sem_out,
):
    s = lax.axis_index("section")
    d = lax.axis_index("dp")
    z, x, c = d // 8, (d // 2) % 4, d % 2
    nxt, prv = (s + 1) % NS, (s + NS - 1) % NS

    def dev(sec, dz, dx, core):
        return (sec, ((z + dz) % NZ) * 8 + ((x + dx) % NX) * 2 + core)

    sibling = dev(s, 0, 0, 1 - c)

    def remote(src, dst, send, recv, target):
        return pltpu.make_async_remote_copy(
            src_ref=src, dst_ref=dst, send_sem=send, recv_sem=recv,
            device_id=target, device_id_type=MESH,
        )

    def piece_of(j):
        dz, dx = j // NX, j % NX
        return ((z + NZ - dz) % NZ) * NX + (x + NX - dx) % NX

    in_fresh = pltpu.make_async_copy(fresh, fresh_v, sem_in.at[0])
    in_carried = pltpu.make_async_copy(carried.at[0], carried_v, sem_in.at[1])
    in_gain = pltpu.make_async_copy(gain, gain_v, sem_in.at[2])
    in_taps = pltpu.make_async_copy(taps_hbm.at[0], taps_v, sem_in.at[3])
    in_long = pltpu.make_async_copy(long_hbm.at[0], long_v, sem_in.at[4])
    in_decay = pltpu.make_async_copy(decay_hbm, decay_v, sem_in.at[5])
    in_fresh.start()
    in_carried.start()

    barrier = pltpu.get_barrier_semaphore()
    peers = [dev(s, dz, 0, c) for dz in range(1, NZ)]
    peers += [dev(s, 0, dx, c) for dx in range(1, NX)]
    peers += [sibling]
    peers += [dev(nxt, dz, 0, c) for dz in range(NZ)]
    peers += [dev(prv, dz, 0, c) for dz in range(NZ)]
    for peer in peers:
        pl.semaphore_signal(barrier, inc=1, device_id=peer, device_id_type=MESH)
    in_gain.start()
    in_taps.start()
    in_long.start()
    in_decay.start()

    in_fresh.wait()
    in_carried.wait()
    first = s == 0
    acts[0, 0] = jnp.where(first, fresh_v[0], carried_v[...])
    pl.semaphore_wait(barrier, len(peers))

    def phase_one(buf, src, send, recv, sec, own):
        for dz in ((0,) if own else ()) + Z_ORDER:
            remote(src, buf.at[dz * NX], send, recv.at[dz * NX], dev(sec, dz, 0, c)).start()

    def arrived(buf, recv, j):
        remote(buf.at[j], buf.at[j], recv.at[j], recv.at[j], sibling).wait_recv()

    def phase_two(buf, send, recv, own):
        for dz in (0,) + Z_ORDER:
            j = dz * NX
            if dz or own:
                arrived(buf, recv, j)
            for dx in X_ORDER:
                remote(buf.at[j], buf.at[j + dx], send, recv.at[j + dx], dev(s, 0, dx, c)).start()

    def drain(buf, send, count):
        pltpu.make_async_copy(buf.at[pl.ds(0, count)], buf.at[pl.ds(0, count)], send).wait()

    phase_one(acts.at[0], acts.at[0, 0], a_send.at[0], a_recv.at[0], s, False)

    @pl.loop(0, NP)
    def _(j):
        col = pl.multiple_of(piece_of(j) * 256 + c * 128, 128)
        other = pl.multiple_of(piece_of(j) * 256 + (1 - c) * 128, 128)
        to = pl.multiple_of(j * 128, 128)
        pltpu.make_async_copy(
            w_in.at[0, :, :, pl.ds(col, 128)], w1.at[0, :, :, pl.ds(to, 128)], sem_w.at[0]
        ).start()
        remote(
            w_in.at[0, :, :, pl.ds(other, 128)], w1.at[1, :, :, pl.ds(to, 128)],
            sem_wsend.at[0], sem_wrecv.at[0], sibling,
        ).start()

    own_out = pltpu.make_async_copy(w_out.at[:, c], w2raw.at[0], sem_w.at[1])
    other_out = remote(w_out.at[:, 1 - c], w2raw.at[1], sem_wsend.at[1], sem_wrecv.at[1], sibling)
    own_out.start()
    other_out.start()

    phase_two(acts.at[0], a_send.at[0], a_recv.at[0], False)

    lane = lax.broadcasted_iota(jnp.int32, (64, 128), 1)
    in_taps.wait()
    in_long.wait()
    in_decay.wait()
    in_gain.wait()
    taps_sq[...] = jnp.zeros_like(taps_sq)
    for i in range(3):
        taps_sq[pl.ds(i * 64, 64), pl.ds(0, 3)] = taps_v[i]
    for half in range(2):
        turned = taps_sq[pl.ds(half * 128, 128), :].T
        taps_row[:, pl.ds(half * 128, 128)] = turned[0:8]
    long_tall = jnp.concatenate([long_v[...], long_v[...]], axis=0).T
    decay_v2 = jnp.concatenate([decay_v[...], decay_v[...]], axis=1)
    lag = lax.broadcasted_iota(jnp.int32, (64, 128), 0) + jnp.where(lane < 64, 0, 64)
    long_row[...] = jnp.where(lane < 64, long_tall[0:64], long_tall[64:128]) * jnp.exp(
        -decay_v2 * lag.astype(F32)
    )
    u_pad[pl.ds(0, 8), :] = jnp.zeros((8, 256), F32)
    p_pad[pl.ds(0, 64), :] = jnp.zeros((64, 128), F32)

    own_out.wait()
    other_out.wait_recv()
    for o in range(2):
        for jp in range(NP // 2):
            two = jnp.concatenate(
                [w2raw[o, piece_of(2 * jp)], w2raw[o, piece_of(2 * jp + 1)]], axis=0
            )
            w2[pl.ds(o * 128, 128), pl.ds(jp * 128, 128)] = two.astype(F32).T.astype(BF16)

    pltpu.make_async_copy(w1.at[0], w1.at[0], sem_w.at[0]).wait()
    remote(w1.at[1], w1.at[1], sem_wsend.at[0], sem_wrecv.at[0], sibling).wait_recv()

    lane128 = lax.broadcasted_iota(jnp.int32, (128, 128), 1)
    low = lane128 < 64

    for k in range(TICKS):
        buf, recv = acts.at[k], a_recv.at[k]
        if k:
            phase_two(buf, a_send.at[k], recv, True)
        squares = jnp.zeros((SEQ, FD), F32)
        slabs = (0,) + Z_ORDER
        for g in range(NZ // GROUP):
            keys = []
            for dz in slabs[g * GROUP:(g + 1) * GROUP]:
                for dx in (0,) + X_ORDER:
                    j = dz * NX + dx
                    if dx:
                        arrived(buf, recv, j)
                    wide = buf[j].astype(F32)
                    col = pl.multiple_of(piece_of(j) * 256 + c * 128, 128)
                    normed[:, pl.ds(j * 128, 128)] = (wide * gain_v[:, pl.ds(col, 128)]).astype(BF16)
                    squares = squares + wide * wide
                keys.append(dz)
            for o in range(2):
                part = None
                for dz in keys:
                    cols = pl.ds(dz * NX * 128, NX * 128)
                    w = w1[o, :, :, cols].reshape(3 * CD, NX * 128)
                    term = lax.dot_general(
                        normed[:, cols], w, (((1,), (1,)), ((), ())), preferred_element_type=F32
                    )
                    part = term if part is None else part + term
                cols192 = pl.ds(0, 192)
                if g == 0:
                    acc[o, :, cols192] = part
                else:
                    acc[o, :, cols192] = acc[o, :, cols192] + part
        row_sq = jnp.sum(squares, axis=1, keepdims=True)
        acc[1, :, pl.ds(192, 64)] = jnp.broadcast_to(row_sq, (SEQ, 64))
        swap = remote(acc.at[1], acc_in.at[k], x_send.at[2 * k], x_recv.at[2 * k], sibling)
        swap.start()
        swap.wait_recv()
        total_sq = row_sq + acc_in[k, :, pl.ds(192, 1)]
        factor = lax.rsqrt(total_sq / D + EPS)
        u_pad[pl.ds(8, SEQ), :] = (acc[0] + acc_in[k]) * factor
        mixed = taps_row[0:1, :] * u_pad[pl.ds(8, SEQ), :]
        for j in range(1, 3):
            mixed = mixed + taps_row[j:j + 1, :] * u_pad[pl.ds(8 - j, SEQ), :]
        left, right = mixed[:, 0:128], mixed[:, 128:256]
        p_low = pltpu.roll(left, 64, 1) * right
        p_high = left * pltpu.roll(right, 64, 1)
        p_pad[pl.ds(64, 64), :] = jnp.where(low[0:64], p_low[0:64], 0.0)
        p_pad[pl.ds(128, 64), :] = jnp.where(low[0:64], p_low[64:128], p_high[0:64])
        conv = jnp.zeros((SEQ, 128), F32)
        for j in range(64):
            conv = conv + long_row[j:j + 1, :] * p_pad[pl.ds(64 - j, SEQ), :]
        y = left * (conv + pltpu.roll(conv, 64, 1))
        gbuf, grecv = gated.at[k], y_recv.at[k]
        gated[k, 0] = y.T[0:64].astype(BF16)
        swap.wait_send()

        phase_one(gbuf, gbuf.at[0], y_send.at[k], grecv, s, False)
        phase_two(gbuf, y_send.at[k], grecv, False)
        total = None
        for g in range(NZ // GROUP):
            for dz in slabs[g * GROUP:(g + 1) * GROUP]:
                for dx in X_ORDER:
                    arrived(gbuf, grecv, dz * NX + dx)
            for dz in slabs[g * GROUP:(g + 1) * GROUP]:
                rhs = gated[k, pl.ds(dz * NX, NX)].reshape(NX * CD, SEQ)
                term = jnp.dot(
                    w2[:, pl.ds(dz * NX * CD, NX * CD)], rhs, preferred_element_type=F32
                )
                total = term if total is None else total + term
        fin_out[...] = total[128:256]
        swap2 = remote(fin_out, fin_in.at[k], x_send.at[2 * k + 1], x_recv.at[2 * k + 1], sibling)
        swap2.start()
        swap2.wait_recv()
        final = (total[0:128] + fin_in[k]).T + acts[k, 0].astype(F32)
        final = final.astype(BF16)
        result[k] = final
        if k + 1 < TICKS:
            produced[k] = jnp.where(s == NS - 1, fresh_v[k + 1], final)
            phase_one(
                acts.at[k + 1], produced.at[k], a_send.at[k + 1], a_recv.at[k + 1], nxt, True
            )
        swap2.wait_send()

    put = pltpu.make_async_copy(result, out.at[0], sem_out)
    put.start()
    pltpu.make_async_copy(w1.at[0], w1.at[0], sem_wsend.at[0]).wait()
    other_out.wait_send()
    for k in range(TICKS):
        drain(acts.at[k], a_send.at[k], NP if k else NP - 1)
        drain(gated.at[k], y_send.at[k], NP - 1)
    put.wait()


def body(fresh_acts, carried, norm_gain, w_in, short_filter, filter_taps, decay_rate, w_out):
    w_out4 = w_out.reshape(NP, 2, CD, FD)
    any_spec = pl.BlockSpec(memory_space=pl.ANY)
    dma = pltpu.SemaphoreType.DMA
    return pl.pallas_call(
        kernel,
        name="relay",
        out_shape=jax.ShapeDtypeStruct((1, TICKS, SEQ, FD), BF16),
        in_specs=[any_spec] * 8,
        out_specs=any_spec,
        scratch_shapes=[
            pltpu.VMEM((TICKS, NP, SEQ, FD), BF16),
            pltpu.VMEM((TICKS, NP, CD, SEQ), BF16),
            pltpu.VMEM((TICKS - 1, SEQ, FD), BF16),
            pltpu.VMEM((TICKS, SEQ, FD), BF16),
            pltpu.VMEM((2, 3, CD, NP * 128), BF16),
            pltpu.VMEM((2, NP, CD, FD), BF16),
            pltpu.VMEM((256, NP * CD), BF16),
            pltpu.VMEM((1, D), F32),
            pltpu.VMEM((TICKS, SEQ, FD), BF16),
            pltpu.VMEM((SEQ, FD), BF16),
            pltpu.VMEM((3, CD, 3), F32),
            pltpu.VMEM((CD, 128), F32),
            pltpu.VMEM((1, CD), F32),
            pltpu.VMEM((256, 128), F32),
            pltpu.VMEM((8, 256), F32),
            pltpu.VMEM((64, 128), F32),
            pltpu.VMEM((SEQ, NP * 128), BF16),
            pltpu.VMEM((2, SEQ, 256), F32),
            pltpu.VMEM((TICKS, SEQ, 256), F32),
            pltpu.VMEM((8 + SEQ, 256), F32),
            pltpu.VMEM((64 + SEQ, 128), F32),
            pltpu.VMEM((FD, SEQ), F32),
            pltpu.VMEM((TICKS, FD, SEQ), F32),
            dma((6,)),
            dma((2,)),
            dma((2,)),
            dma((2,)),
            dma((TICKS,)),
            dma((TICKS, NP)),
            dma((TICKS,)),
            dma((TICKS, NP)),
            dma((2 * TICKS,)),
            dma((2 * TICKS,)),
            dma(()),
        ],
        compiler_params=pltpu.CompilerParams(
            collective_id=0, has_side_effects=True, vmem_limit_bytes=56 << 20
        ),
    )(fresh_acts, carried, norm_gain, w_in, short_filter, filter_taps, decay_rate, w_out4)


def solution(mesh):
    return jax.shard_map(
        body,
        mesh=mesh,
        in_specs=(
            P(None, None, "dp"),
            P("section", None, "dp"),
            P("section", None),
            P("section", None, "dp", None),
            P("section", None, "dp", None),
            P("section", "dp", None),
            P("section", "dp"),
            P("section", None, "dp"),
        ),
        out_specs=P("section", None, None, "dp"),
        check_vma=False,
    )
```

time: 633 us -> 112 us (0.18)
  waiting for transfers between devices: 564 us -> 0 us
  Pallas kernels: 0 us -> 109 us
  matrix products: 31.2 us -> 0 us
  between operations: 13.7 us -> 0.01 us
  other arithmetic: 8.37 us -> 0 us
  starting transfers between devices: 6.59 us -> 0 us
    all_gather x6 -> x0, waiting for transfers between devices: 470 us -> none  [the longest x3 245 us: body(): lax.all_gather(y_local, 'dp', axis=1, tiled=True)]
    pallas_call x0 -> x1, Pallas kernels: none -> 109 us  [body(): pl.pallas_call(kernel, name='relay', out_shape=jax.ShapeDtypeStruct((1, T...]
    ppermute x2 -> x0, waiting for transfers between devices: 94.2 us -> none  [shifted(): return lax.ppermute(value, axis, pairs)]
    dot_general x10 -> x0, matrix products: 31.2 us -> none  [the longest x3 11 us: mixing(): jnp.einsum('cts,sc->tc', toeplitz, product, precision=lax.Precision.HIGHEST)]
    ppermute x2 -> x0, starting transfers between devices: 6.38 us -> none  [shifted(): return lax.ppermute(value, axis, pairs)]
  transfers between devices with their start and end apart: 8 -> 0, of which waited for: 8 -> 0; matrix products, arithmetic and copies ran while one was open for 2% -> 0% of each run, Pallas kernels for 0% -> 0%
where the time goes in v1:
time: 112 us
  Pallas kernels  109 us (97%)
  local copies, waits for them, and re-layouts  2.98 us (3%)
    pallas_call x1, Pallas kernels, body(): pl.pallas_call(kernel, name='relay', out_shape=jax.ShapeDtypeStruct((1, T...  109 us
    unnamed x2, local copies, waits for them, and re-layouts  2.98 us

profile of v1, /device:TPU:1, one launch (start us, length us, event | category | flops | bytes accessed | tf_op | source)
XLA Modules:
  0.0 111.7 jit_solution(17994830763427875129)
XLA Ops:
  0.0 1.4 %copy.9.taps_hbm = f32[1,3,64,3]{3,2,1,0:T(8,128)} copy(f32[1,3,64,3]{2,0,3,1:T(1,128)} %param.12) | data formatting | bytes 4608 | tf_op args[4]
  1.4 108.7 %relay.1 = bf16[1,3,128,128]{3,2,1,0:T(8,128)(2,1)} custom-call(bf16[3,128,128]{2,1,0:T(8,128)(2,1)} %fresh.1, bf16[1,128,128]{2,1,0:T(8,128)(2,1)} %carried.1, f32[1,8192]{1,0:T(1,128)} %gain.1, bf16[1,3,64,8192]{3,2,1,0:T(8,128)(2,1)} %w_in.1, f32[1,3,64,3]{3,2,1,0:T(8,128)} %copy.9.taps_hbm, f32[1,64,128]{2,1,0:T(8,128)} %long_hbm.1, f32[1,64]{1,0:T(1,128)} %decay_hbm.1, ...), custom_call_target="tpu_custom_call" | custom-call | tf_op jit(solution)/shard_map/relay/pallas_call | solution.py:247
  110.1 1.5 %copy.11 = bf16[1,3,128,128]{3,2,1,0:T(8,128)(2,1)} copy(bf16[1,3,128,128]{3,2,1,0:T(8,128)(2,1)} %relay.1) | data formatting | bytes 196608

commit v2 on v1

v2 whole, which is shorter than its diff:
```python
import jax
import jax.numpy as jnp
from jax import lax
from jax.experimental import pallas as pl
from jax.experimental.pallas import tpu as pltpu
from jax.sharding import PartitionSpec as P

EPS = 1e-06
MESH = pl.DeviceIdType.MESH
F32 = jnp.float32
BF16 = jnp.bfloat16

NZ, NX, NS = 8, 4, 8
NP = NZ * NX
TICKS, SEQ, FD, CD, D = 3, 128, 128, 64, 8192
NH, HT = 2, 64
Z_ORDER = (1, 7, 2, 6, 3, 5, 4)
X_ORDER = (1, 3, 2)
SLABS = (0,) + Z_ORDER


def kernel(
    fresh, carried, gain, w_in, taps_hbm, long_hbm, decay_hbm, w_out, out,
    acts, gated, produced, result, w1, w2raw, w2, gain_v, fresh_v, carried_v,
    taps_v, long_v, decay_v, taps_row, long_row, normed, acc, acc_in, u_pad, p_pad, fin_out, fin_in,
    sem_in, sem_w, sem_wsend, sem_wrecv, a_send, a_recv, y_send, y_recv, u_send, u_recv, f_send, f_recv, sem_out,
):
    s = lax.axis_index("section")
    d = lax.axis_index("dp")
    z, x, c = d // 8, (d // 2) % 4, d % 2
    nxt, prv = (s + 1) % NS, (s + NS - 1) % NS

    def dev(sec, dz, dx, core):
        return (sec, ((z + dz) % NZ) * 8 + ((x + dx) % NX) * 2 + core)

    sibling = dev(s, 0, 0, 1 - c)

    def remote(src, dst, send, recv, target):
        return pltpu.make_async_remote_copy(
            src_ref=src, dst_ref=dst, send_sem=send, recv_sem=recv,
            device_id=target, device_id_type=MESH,
        )

    def piece_of(j):
        dz, dx = j // NX, j % NX
        return ((z + NZ - dz) % NZ) * NX + (x + NX - dx) % NX

    in_fresh = pltpu.make_async_copy(fresh, fresh_v, sem_in.at[0])
    in_carried = pltpu.make_async_copy(carried.at[0], carried_v, sem_in.at[1])
    in_gain = pltpu.make_async_copy(gain, gain_v, sem_in.at[2])
    in_taps = pltpu.make_async_copy(taps_hbm, taps_v, sem_in.at[3])
    in_long = pltpu.make_async_copy(long_hbm.at[0], long_v, sem_in.at[4])
    in_decay = pltpu.make_async_copy(decay_hbm, decay_v, sem_in.at[5])
    in_fresh.start()
    in_carried.start()

    barrier = pltpu.get_barrier_semaphore()
    peers = [dev(s, dz, 0, c) for dz in range(1, NZ)]
    peers += [dev(s, 0, dx, c) for dx in range(1, NX)]
    peers += [sibling]
    peers += [dev(nxt, dz, 0, c) for dz in range(NZ)]
    peers += [dev(prv, dz, 0, c) for dz in range(NZ)]
    for peer in peers:
        pl.semaphore_signal(barrier, inc=1, device_id=peer, device_id_type=MESH)
    in_gain.start()
    in_taps.start()
    in_long.start()
    in_decay.start()

    in_fresh.wait()
    in_carried.wait()
    start = jnp.where(s == 0, fresh_v[0], carried_v[...])
    for h in range(NH):
        acts[0, h, 0] = start[h * HT:(h + 1) * HT]
    pl.semaphore_wait(barrier, len(peers))

    def phase_one(buf, src, send, recv, sec, own):
        for dz in SLABS if own else Z_ORDER:
            remote(src, buf.at[dz * NX], send, recv.at[dz * NX], dev(sec, dz, 0, c)).start()

    def arrived(buf, recv, j):
        remote(buf.at[j], buf.at[j], recv.at[j], recv.at[j], sibling).wait_recv()

    def phase_two(buf, send, recv, own, slabs):
        for dz in slabs:
            j = dz * NX
            if dz or own:
                arrived(buf, recv, j)
            for dx in X_ORDER:
                remote(buf.at[j], buf.at[j + dx], send, recv.at[j + dx], dev(s, 0, dx, c)).start()

    def drain(buf, send, count):
        pltpu.make_async_copy(buf.at[pl.ds(0, count)], buf.at[pl.ds(0, count)], send).wait()

    for h in range(NH):
        phase_one(acts.at[0, h], acts.at[0, h, 0], a_send.at[0, h], a_recv.at[0, h], s, False)

    @pl.loop(0, NP)
    def _(j):
        col = pl.multiple_of(piece_of(j) * 256 + c * 128, 128)
        other = pl.multiple_of(piece_of(j) * 256 + (1 - c) * 128, 128)
        to = pl.multiple_of(j * 128, 128)
        pltpu.make_async_copy(
            w_in.at[0, :, :, pl.ds(col, 128)], w1.at[0, :, :, pl.ds(to, 128)], sem_w.at[0]
        ).start()
        remote(
            w_in.at[0, :, :, pl.ds(other, 128)], w1.at[1, :, :, pl.ds(to, 128)],
            sem_wsend.at[0], sem_wrecv.at[0], sibling,
        ).start()

    own_out = pltpu.make_async_copy(w_out.at[:, c], w2raw.at[0], sem_w.at[1])
    other_out = remote(w_out.at[:, 1 - c], w2raw.at[1], sem_wsend.at[1], sem_wrecv.at[1], sibling)
    own_out.start()
    other_out.start()

    for h in range(NH):
        phase_two(acts.at[0, h], a_send.at[0, h], a_recv.at[0, h], False, SLABS)

    lane = lax.broadcasted_iota(jnp.int32, (64, 128), 1)
    low = lane < 64
    in_taps.wait()
    in_long.wait()
    in_decay.wait()
    in_gain.wait()
    for j in range(3):
        taps_row[pl.ds(j, 1), pl.ds(0, 128)] = jnp.concatenate([taps_v[0, j], taps_v[1, j]], axis=1)
        taps_row[pl.ds(j, 1), pl.ds(128, 128)] = jnp.concatenate([taps_v[2, j], taps_v[2, j]], axis=1)
    long_tall = jnp.concatenate([long_v[...], long_v[...]], axis=0).T
    decay_v2 = jnp.concatenate([decay_v[...], decay_v[...]], axis=1)
    lag = lax.broadcasted_iota(jnp.int32, (64, 128), 0) + jnp.where(low, 0, 64)
    long_row[...] = jnp.where(low, long_tall[0:64], long_tall[64:128]) * jnp.exp(
        -decay_v2 * lag.astype(F32)
    )

    own_out.wait()
    other_out.wait_recv()
    for o in range(2):
        for jp in range(NZ):
            pieces = [w2raw[o, piece_of(NX * jp + i)].astype(F32) for i in range(NX)]
            for part in range(2):
                four = jnp.concatenate([p[part * 32:part * 32 + 32] for p in pieces], axis=0)
                w2[pl.ds(part * 256 + o * 128, 128), pl.ds(jp * 128, 128)] = four.T.astype(BF16)

    pltpu.make_async_copy(w1.at[0], w1.at[0], sem_w.at[0]).wait()
    remote(w1.at[1], w1.at[1], sem_wsend.at[0], sem_wrecv.at[0], sibling).wait_recv()

    for k in range(TICKS):
        u_pad[k, pl.ds(0, 8), :] = jnp.zeros((8, 256), F32)
        p_pad[k, pl.ds(0, 64), :] = jnp.zeros((64, 128), F32)

    swaps = {}

    def spread(k, h, slabs):
        phase_two(acts.at[k, h], a_send.at[k, h], a_recv.at[k, h], k > 0, slabs)

    def project(k, h):
        buf, recv = acts.at[k, h], a_recv.at[k, h]
        squares = jnp.zeros((HT, FD), F32)
        for n, dz in enumerate(SLABS):
            for dx in (0,) + X_ORDER:
                j = dz * NX + dx
                if dx:
                    arrived(buf, recv, j)
                wide = buf[j].astype(F32)
                col = pl.multiple_of(piece_of(j) * 256 + c * 128, 128)
                normed[h, :, pl.ds(j * 128, 128)] = (wide * gain_v[:, pl.ds(col, 128)]).astype(BF16)
                squares = squares + wide * wide
            cols = pl.ds(dz * NX * 128, NX * 128)
            lhs = normed[h, :, cols]
            for o in range(2):
                w = w1[o, :, :, cols].reshape(3 * CD, NX * 128)
                term = lax.dot_general(
                    lhs, w, (((1,), (1,)), ((), ())), preferred_element_type=F32
                )
                if n == 0:
                    acc[k, h, o, :, pl.ds(0, 192)] = term
                else:
                    acc[k, h, o, :, pl.ds(0, 192)] = acc[k, h, o, :, pl.ds(0, 192)] + term
        row_sq = jnp.sum(squares, axis=1, keepdims=True)
        for o in range(2):
            acc[k, h, o, :, pl.ds(192, 64)] = jnp.broadcast_to(row_sq, (HT, 64))
        swaps[k, h, 0] = remote(
            acc.at[k, h, 1], acc_in.at[k, h], u_send.at[k, h], u_recv.at[k, h], sibling
        )
        swaps[k, h, 0].start()

    def mix(k, h):
        swaps[k, h, 0].wait_recv()
        both = acc[k, h, 0] + acc_in[k, h]
        factor = lax.rsqrt(both[:, 192:193] / D + EPS)
        row = 8 + h * HT
        u_pad[k, pl.ds(row, HT), :] = both * factor
        mixed = taps_row[0:1, :] * u_pad[k, pl.ds(row, HT), :]
        for j in range(1, 3):
            mixed = mixed + taps_row[j:j + 1, :] * u_pad[k, pl.ds(row - j, HT), :]
        left, right = mixed[:, 0:128], mixed[:, 128:256]
        p_low = pltpu.roll(left, 64, 1) * right
        if h == 0:
            p_pad[k, pl.ds(64, 64), :] = jnp.where(low, p_low, 0.0)
            p_pad[k, pl.ds(128, 64), :] = jnp.where(low, 0.0, left * pltpu.roll(right, 64, 1))
        else:
            p_pad[k, pl.ds(128, 64), :] = jnp.where(low, p_low, p_pad[k, pl.ds(128, 64), :])
        conv = jnp.zeros((HT, 128), F32)
        for j in range(64):
            conv = conv + long_row[j:j + 1, :] * p_pad[k, pl.ds(64 + h * HT - j, HT), :]
        y = left * (conv + pltpu.roll(conv, 64, 1))
        tall = jnp.concatenate([y, pltpu.roll(y, 96, 1)], axis=0).T
        gated[k, h, 0] = tall[0:32].astype(BF16)
        phase_one(gated.at[k, h], gated.at[k, h, 0], y_send.at[k, h], y_recv.at[k, h], s, False)

    def spread_gated(k, h, slabs):
        phase_two(gated.at[k, h], y_send.at[k, h], y_recv.at[k, h], False, slabs)

    def combine(k, h):
        buf, recv = gated.at[k, h], y_recv.at[k, h]
        total = None
        for g in range(4):
            for dz in SLABS[2 * g:2 * g + 2]:
                for dx in X_ORDER:
                    arrived(buf, recv, dz * NX + dx)
            for dz in SLABS[2 * g:2 * g + 2]:
                rhs = gated[k, h, pl.ds(dz * NX, NX)].reshape(NX * 32, 128)
                term = jnp.dot(w2[:, pl.ds(dz * 128, 128)], rhs, preferred_element_type=F32)
                total = term if total is None else total + term
        folded = total[0:256] + pltpu.roll(total[256:512], 64, 1)
        fin_out[k, h, 0] = folded[0:128].T[0:HT]
        fin_out[k, h, 1] = folded[128:256].T[0:HT]
        swaps[k, h, 1] = remote(
            fin_out.at[k, h, 1], fin_in.at[k, h], f_send.at[k, h], f_recv.at[k, h], sibling
        )
        swaps[k, h, 1].start()

    def finish(k, h):
        swaps[k, h, 1].wait_recv()
        rows = pl.ds(h * HT, HT)
        final = (fin_out[k, h, 0] + fin_in[k, h]) + acts[k, h, 0].astype(F32)
        final = final.astype(BF16)
        result[k, rows] = final
        if k + 1 < TICKS:
            produced[k, h] = jnp.where(s == NS - 1, fresh_v[k + 1, rows], final)
            phase_one(
                acts.at[k + 1, h], produced.at[k, h], a_send.at[k + 1, h], a_recv.at[k + 1, h], nxt, True
            )

    for k in range(TICKS):
        if k:
            spread(k, 0, SLABS)
            spread(k, 1, SLABS)
        project(k, 0)
        mix(k, 0)
        project(k, 1)
        mix(k, 1)
        spread_gated(k, 0, SLABS)
        spread_gated(k, 1, SLABS)
        combine(k, 0)
        finish(k, 0)
        combine(k, 1)
        finish(k, 1)

    put = pltpu.make_async_copy(result, out.at[0], sem_out)
    put.start()
    pltpu.make_async_copy(w1.at[0], w1.at[0], sem_wsend.at[0]).wait()
    other_out.wait_send()
    for swap in swaps.values():
        swap.wait_send()
    for k in range(TICKS):
        for h in range(NH):
            drain(acts.at[k, h], a_send.at[k, h], NP if k else NP - 1)
            drain(gated.at[k, h], y_send.at[k, h], NP - 1)
    put.wait()


def body(fresh_acts, carried, norm_gain, w_in, short_filter, filter_taps, decay_rate, w_out):
    w_out4 = w_out.reshape(NP, 2, CD, FD)
    taps = jnp.transpose(short_filter, (1, 3, 0, 2))
    any_spec = pl.BlockSpec(memory_space=pl.ANY)
    dma = pltpu.SemaphoreType.DMA
    return pl.pallas_call(
        kernel,
        name="relay",
        out_shape=jax.ShapeDtypeStruct((1, TICKS, SEQ, FD), BF16),
        in_specs=[any_spec] * 8,
        out_specs=any_spec,
        scratch_shapes=[
            pltpu.VMEM((TICKS, NH, NP, HT, FD), BF16),
            pltpu.VMEM((TICKS, NH, NP, 32, 128), BF16),
            pltpu.VMEM((TICKS - 1, NH, HT, FD), BF16),
            pltpu.VMEM((TICKS, SEQ, FD), BF16),
            pltpu.VMEM((2, 3, CD, NP * 128), BF16),
            pltpu.VMEM((2, NP, CD, FD), BF16),
            pltpu.VMEM((512, NP * 32), BF16),
            pltpu.VMEM((1, D), F32),
            pltpu.VMEM((TICKS, SEQ, FD), BF16),
            pltpu.VMEM((SEQ, FD), BF16),
            pltpu.VMEM((3, 3, 1, CD), F32),
            pltpu.VMEM((CD, 128), F32),
            pltpu.VMEM((1, CD), F32),
            pltpu.VMEM((8, 256), F32),
            pltpu.VMEM((64, 128), F32),
            pltpu.VMEM((NH, HT, NP * 128), BF16),
            pltpu.VMEM((TICKS, NH, 2, HT, 256), F32),
            pltpu.VMEM((TICKS, NH, HT, 256), F32),
            pltpu.VMEM((TICKS, 8 + SEQ, 256), F32),
            pltpu.VMEM((TICKS, 64 + SEQ, 128), F32),
            pltpu.VMEM((TICKS, NH, 2, HT, FD), F32),
            pltpu.VMEM((TICKS, NH, HT, FD), F32),
            dma((6,)),
            dma((2,)),
            dma((2,)),
            dma((2,)),
            dma((TICKS, NH)),
            dma((TICKS, NH, NP)),
            dma((TICKS, NH)),
            dma((TICKS, NH, NP)),
            dma((TICKS, NH)),
            dma((TICKS, NH)),
            dma((TICKS, NH)),
            dma((TICKS, NH)),
            dma(()),
        ],
        compiler_params=pltpu.CompilerParams(
            collective_id=0, has_side_effects=True, vmem_limit_bytes=56 << 20
        ),
    )(fresh_acts, carried, norm_gain, w_in, taps, filter_taps, decay_rate, w_out4)


def solution(mesh):
    return jax.shard_map(
        body,
        mesh=mesh,
        in_specs=(
            P(None, None, "dp"),
            P("section", None, "dp"),
            P("section", None),
            P("section", None, "dp", None),
            P("section", None, "dp", None),
            P("section", "dp", None),
            P("section", "dp"),
            P("section", None, "dp"),
        ),
        out_specs=P("section", None, None, "dp"),
        check_vma=False,
    )
```

time: 112 us -> 102 us (0.911)
  Pallas kernels: 109 us -> 100 us
  local copies, waits for them, and re-layouts: 2.98 us -> 1.54 us
    pallas_call x1, Pallas kernels: 109 us -> 100 us  [body(): pl.pallas_call(kernel, name='relay', out_shape=jax.ShapeDtypeStruct((1, T...]
    unnamed x2 -> x1, local copies, waits for them, and re-layouts: 2.98 us -> 1.54 us
where the time goes in v2:
time: 102 us
  Pallas kernels  100 us (98%)
  local copies, waits for them, and re-layouts  1.54 us (2%)
    pallas_call x1, Pallas kernels, body(): pl.pallas_call(kernel, name='relay', out_shape=jax.ShapeDtypeStruct((1, T...  100 us

profile of v2, /device:TPU:1, one launch (start us, length us, event | category | flops | bytes accessed | tf_op | source)
XLA Modules:
  0.0 102.0 jit_solution(5439559958448818590)
XLA Ops:
  0.0 100.4 %relay.1 = bf16[1,3,128,128]{3,2,1,0:T(8,128)(2,1)} custom-call(bf16[3,128,128]{2,1,0:T(8,128)(2,1)} %fresh.1, bf16[1,128,128]{2,1,0:T(8,128)(2,1)} %carried.1, f32[1,8192]{1,0:T(1,128)} %gain.1, bf16[1,3,64,8192]{3,2,1,0:T(8,128)(2,1)} %w_in.1, f32[3,3,1,64]{3,2,1,0:T(1,128)} %bitcast.3, f32[1,64,128]{2,1,0:T(8,128)} %long_hbm.1, f32[1,64]{1,0:T(1,128)} %decay_hbm.1, ...), custom_call_target="tpu_custom_call" | custom-call | tf_op jit(solution)/shard_map/relay/pallas_call | solution.py:278
  100.4 1.5 %copy.10 = bf16[1,3,128,128]{3,2,1,0:T(8,128)(2,1)} copy(bf16[1,3,128,128]{3,2,1,0:T(8,128)(2,1)} %relay.1) | data formatting | bytes 196608

commit v3 on v0

v3 whole, which is shorter than its diff:
```python
import jax
import jax.numpy as jnp
from jax import lax
from jax.experimental import pallas as pl
from jax.experimental.pallas import tpu as pltpu
from jax.sharding import PartitionSpec as P

EPS = 1e-06
MESH = pl.DeviceIdType.MESH
F32 = jnp.float32
BF16 = jnp.bfloat16

NZ, NX, NS = 8, 4, 8
NP = NZ * NX
TICKS, SEQ, FD, CD, D = 3, 128, 128, 64, 8192
NH, BT = 2, 32
Z_ORDER = (1, 7, 2, 6, 3, 5, 4)
X_ORDER = (2, 1, 3)
SLABS = (0,) + Z_ORDER
NEAR = (1, 7, 2, 6)
DIRECT = ((0, 2), (1, 0), (7, 0), (2, 0), (6, 0), (3, 0), (5, 0), (4, 0))
STEPS = (0, 1, 7, "across", 2, 6, 3, 5, 4)


def kernel(
    fresh, carried, gain, w_in, taps_hbm, long_hbm, decay_hbm, w_out, out,
    acts, gated, produced, final_v, result, w1, w2, gain_v, fresh_v, carried_v,
    taps_v, long_v, decay_v, taps_row, long_row, u_pad, p_pad,
    sem_in, sem_own, sem_xsend, sem_xrecv, a_send, a_recv, y_send, y_recv,
    u_send, u_recv, p_send, p_recv, o_send, o_recv, sem_out,
):
    s = lax.axis_index("section")
    d = lax.axis_index("dp")
    z, x, c = d // 8, (d // 2) % 4, d % 2
    nxt, prv = (s + 1) % NS, (s + NS - 1) % NS

    def dev(sec, dz, dx, core):
        return (sec, ((z + dz) % NZ) * 8 + ((x + dx) % NX) * 2 + core)

    sibling = dev(s, 0, 0, 1 - c)

    def remote(src, dst, send, recv, target):
        return pltpu.make_async_remote_copy(
            src_ref=src, dst_ref=dst, send_sem=send, recv_sem=recv,
            device_id=target, device_id_type=MESH,
        )

    def local(src, dst, sem):
        return pltpu.make_async_copy(src, dst, sem)

    def piece_of(j):
        dz, dx = j // NX, j % NX
        return ((z + NZ - dz) % NZ) * NX + (x + NX - dx) % NX

    mine = pl.ds(pl.multiple_of(c * FD, FD), FD)
    other = pl.ds(pl.multiple_of((1 - c) * FD, FD), FD)

    in_gain = local(gain, gain_v, sem_in.at[0])
    keep = []
    for h in range(NH):
        keep.append(local(carried.at[2 * h + c], carried_v.at[h, :, mine], sem_own.at[0]))
        keep.append(local(fresh.at[0, 2 * h + c], fresh_v.at[0, h, :, mine], sem_own.at[1]))
    for copy in keep:
        copy.start()

    barrier = pltpu.get_barrier_semaphore()
    peers = [sibling]
    for sec in (nxt, prv):
        peers += [dev(sec, dz, 0, c) for dz in range(NZ)]
        peers += [dev(sec, 0, 2, c)]
    peers += [dev(s, dz, 0, c) for dz in range(1, NZ)]
    peers += [dev(s, 0, dx, c) for dx in range(1, NX)]
    for peer in peers:
        pl.semaphore_signal(barrier, inc=1, device_id=peer, device_id_type=MESH)
    in_gain.start()
    pl.semaphore_wait(barrier, len(peers))

    for h in range(NH):
        remote(
            carried.at[2 * h + 1 - c], carried_v.at[h, :, mine], sem_xsend.at[0], sem_xrecv.at[0], sibling
        ).start()
        remote(
            fresh.at[0, 2 * h + 1 - c], fresh_v.at[0, h, :, mine], sem_xsend.at[1], sem_xrecv.at[1], sibling
        ).start()
    pairs = (
        (taps_hbm, taps_v.at[c], 2),
        (long_hbm.at[0], long_v.at[c], 3),
        (decay_hbm, decay_v.at[c], 4),
        (w_in.at[0], w1.at[:, c], 5),
        (w_out, w2.at[:, :, mine], 6),
    )

    def half_wait(sem, ref):
        local(ref, ref, sem).wait()

    half_wait(sem_own.at[0], carried_v.at[:, :, mine])
    half_wait(sem_own.at[1], fresh_v.at[0, :, :, mine])
    half_wait(sem_xrecv.at[0], carried_v.at[:, :, other])
    half_wait(sem_xrecv.at[1], fresh_v.at[0, :, :, other])
    for h in range(NH):
        acts[0, h, 0] = jnp.where(s == 0, fresh_v[0, h], carried_v[h])

    def phase_one(buf, src, send, recv, sec, own):
        for dz, dx in (((0, 0),) if own else ()) + DIRECT:
            j = dz * NX + dx
            remote(src, buf.at[j], send, recv.at[j], dev(sec, dz, dx, c)).start()

    def arrived(buf, recv, j):
        remote(buf.at[j], buf.at[j], recv.at[j], recv.at[j], sibling).wait_recv()

    def phase_two(buf, send, recv, own, slabs):
        for step in slabs:
            if step == "across":
                arrived(buf, recv, 2)
                for dz in NEAR:
                    j = dz * NX + 2
                    remote(buf.at[2], buf.at[j], send, recv.at[j], dev(s, dz, 0, c)).start()
                continue
            j = step * NX
            if step or own:
                arrived(buf, recv, j)
            for dx in X_ORDER:
                if dx == 2 and (step == 0 or step in NEAR):
                    continue
                remote(buf.at[j], buf.at[j + dx], send, recv.at[j + dx], dev(s, 0, dx, c)).start()

    def drain(buf, send, count):
        local(buf.at[pl.ds(0, count)], buf.at[pl.ds(0, count)], send).wait()

    for h in range(NH):
        phase_one(acts.at[0, h], acts.at[0, h, 0], a_send.at[0, h], a_recv.at[0, h], s, False)

    for src, dst, n in pairs:
        local(src, dst, sem_own.at[n]).start()
        remote(src, dst, sem_xsend.at[n], sem_xrecv.at[n], sibling).start()
    for k in range(1, TICKS):
        for h in range(NH):
            local(fresh.at[k, 2 * h + c], fresh_v.at[k, h, :, mine], sem_own.at[7]).start()
            remote(
                fresh.at[k, 2 * h + 1 - c], fresh_v.at[k, h, :, mine], sem_xsend.at[7], sem_xrecv.at[7], sibling
            ).start()

    for h in range(NH):
        phase_two(acts.at[0, h], a_send.at[0, h], a_recv.at[0, h], False, STEPS)

    in_gain.wait()
    for src, dst, n in pairs:
        local(src, dst, sem_own.at[n]).wait()
        remote(src, dst, sem_xsend.at[n], sem_xrecv.at[n], sibling).wait_recv()
    later = pl.ds(1, TICKS - 1)
    half_wait(sem_own.at[7], fresh_v.at[later, :, :, mine])
    half_wait(sem_xrecv.at[7], fresh_v.at[later, :, :, other])

    for i in range(3):
        for j in range(3):
            taps_row[pl.ds(j, 1), pl.ds(i * 128, 128)] = jnp.concatenate(
                [taps_v[0, i, j], taps_v[1, i, j]], axis=1
            )
    tall = jnp.concatenate([long_v[0], long_v[1]], axis=0).T
    decay_all = jnp.concatenate([decay_v[0], decay_v[1]], axis=1)
    lag = lax.broadcasted_iota(jnp.int32, (128, 128), 0).astype(F32)
    long_row[...] = tall * jnp.exp(-decay_all * lag)
    for k in range(TICKS):
        p_pad[k, pl.ds(0, BT), :] = jnp.zeros((BT, 128), F32)

    @pl.when(c == 0)
    def _():
        for k in range(TICKS):
            u_pad[k, 0, pl.ds(0, 8), :] = jnp.zeros((8, 384), F32)

    def tail_copy(k, h, cc):
        to = h + cc
        return remote(
            u_pad.at[k, h, pl.ds(BT, 8)], u_pad.at[k, to, pl.ds(0, 8)],
            u_send.at[k, h], u_recv.at[k, to], sibling,
        )

    def history_copy(k, b):
        rows = pl.ds(BT + b * BT, BT)
        return remote(
            p_pad.at[k, rows], p_pad.at[k, rows], p_send.at[k, b], p_recv.at[k, b], sibling
        )

    def spread(k, h, slabs):
        phase_two(acts.at[k, h], a_send.at[k, h], a_recv.at[k, h], k > 0, slabs)

    def project(k, h):
        buf, recv = acts.at[k, h], a_recv.at[k, h]
        squares = jnp.zeros((BT, 256), F32)
        total = jnp.zeros((BT, 384), F32)
        for dz in SLABS:
            for dx in (0,) + X_ORDER:
                j = dz * NX + dx
                if dx and j != 2:
                    arrived(buf, recv, j)
                wide = buf[j].astype(F32)
                cols = pl.ds(pl.multiple_of(piece_of(j) * 256, 256), 256)
                normed = (wide * gain_v[:, cols]).astype(BF16)
                squares = squares + wide * wide
                w = w1[:, :, :, cols].reshape(384, 256)
                total = total + lax.dot_general(
                    normed, w, (((1,), (1,)), ((), ())), preferred_element_type=F32
                )
        factor = lax.rsqrt(jnp.sum(squares, axis=1, keepdims=True) / D + EPS)
        u_pad[k, h, pl.ds(8, BT), :] = total * factor
        for cc in range(2):
            if h + cc < NH:
                @pl.when(c == cc)
                def _():
                    tail_copy(k, h, cc).start()

    def mix(k, h):
        for cc in range(2):
            b = 2 * h + cc

            @pl.when(c == cc)
            def _():
                if b:
                    tail = u_pad.at[k, h, pl.ds(0, 8)]
                    remote(tail, tail, u_recv.at[k, h], u_recv.at[k, h], sibling).wait_recv()
                mixed = taps_row[0:1, :] * u_pad[k, h, pl.ds(8, BT), :]
                for j in range(1, 3):
                    mixed = mixed + taps_row[j:j + 1, :] * u_pad[k, h, pl.ds(8 - j, BT), :]
                p_pad[k, pl.ds(BT + b * BT, BT), :] = mixed[:, 128:256] * mixed[:, 256:384]
                if b < 3:
                    history_copy(k, b).start()
                if b:
                    history_copy(k, b - 1).wait_recv()
                conv = jnp.zeros((BT, 128), F32)
                for j in range(BT * (b + 1)):
                    conv = conv + long_row[j:j + 1, :] * p_pad[k, pl.ds(BT + b * BT - j, BT), :]
                gated[k, h, 0] = (mixed[:, 0:128] * conv).astype(BF16)

        phase_one(gated.at[k, h], gated.at[k, h, 0], y_send.at[k, h], y_recv.at[k, h], s, False)

    def spread_gated(k, h, slabs):
        phase_two(gated.at[k, h], y_send.at[k, h], y_recv.at[k, h], False, slabs)

    def combine(k, h):
        buf, recv = gated.at[k, h], y_recv.at[k, h]
        total = jnp.zeros((BT, 256), F32)
        for dz in SLABS:
            for dx in X_ORDER:
                if dz or dx != 2:
                    arrived(buf, recv, dz * NX + dx)
            js = [dz * NX + dx for dx in range(NX)]
            lhs = jnp.concatenate([buf[j] for j in js], axis=1)
            rhs = jnp.concatenate([w2[piece_of(j)] for j in js], axis=0)
            total = total + jnp.dot(lhs, rhs, preferred_element_type=F32)
        final = (total + acts[k, h, 0].astype(F32)).astype(BF16)
        if k + 1 < TICKS:
            produced[k, h] = jnp.where(s == NS - 1, fresh_v[k + 1, h], final)
            phase_one(
                acts.at[k + 1, h], produced.at[k, h], a_send.at[k + 1, h], a_recv.at[k + 1, h], nxt, True
            )
        final_v[k, h] = final
        block = 2 * h + c
        result[k, block] = jnp.where(c == 0, final[:, 0:128], final[:, 128:256])
        out_copy(k, h).start()

    def out_copy(k, h):
        block = 2 * h + c
        return remote(
            final_v.at[k, h, :, other], result.at[k, block], o_send.at[k, h], o_recv.at[k, h], sibling
        )

    for k in range(TICKS):
        if k:
            spread(k, 0, STEPS)
            spread(k, 1, STEPS)
        project(k, 0)
        mix(k, 0)
        project(k, 1)
        mix(k, 1)
        spread_gated(k, 0, STEPS)
        spread_gated(k, 1, STEPS)
        combine(k, 0)
        combine(k, 1)

    for k in range(TICKS):
        for h in range(NH):
            out_copy(k, h).wait_recv()
    put = local(result, out, sem_out)
    put.start()
    for src, dst, n in pairs:
        remote(src, dst, sem_xsend.at[n], sem_xrecv.at[n], sibling).wait_send()
    half_wait(sem_xsend.at[0], carried_v.at[:, :, other])
    half_wait(sem_xsend.at[1], fresh_v.at[0, :, :, other])
    half_wait(sem_xsend.at[7], fresh_v.at[later, :, :, other])
    for k in range(TICKS):
        for h in range(NH):
            out_copy(k, h).wait_send()
            drain(acts.at[k, h], a_send.at[k, h], NP if k else NP - 1)
            drain(gated.at[k, h], y_send.at[k, h], NP - 1)
            for cc in range(2):
                if 2 * h + cc < 3:
                    @pl.when(c == cc)
                    def _():
                        tail_copy(k, h, cc).wait_send()
                        history_copy(k, 2 * h + cc).wait_send()
    put.wait()


def body(fresh_acts, carried, norm_gain, w_in, short_filter, filter_taps, decay_rate, w_out):
    blocks = SEQ // BT
    fresh = fresh_acts.reshape(TICKS, blocks, BT, FD)
    waiting = carried.reshape(blocks, BT, FD)
    w_out3 = w_out.reshape(NP, 2 * CD, FD)
    taps = jnp.transpose(short_filter, (1, 3, 0, 2))
    any_spec = pl.BlockSpec(memory_space=pl.ANY)
    dma = pltpu.SemaphoreType.DMA
    made = pl.pallas_call(
        kernel,
        name="relay",
        out_shape=jax.ShapeDtypeStruct((TICKS, blocks, BT, FD), BF16),
        in_specs=[any_spec] * 8,
        out_specs=any_spec,
        scratch_shapes=[
            pltpu.VMEM((TICKS, NH, NP, BT, 256), BF16),
            pltpu.VMEM((TICKS, NH, NP, BT, 128), BF16),
            pltpu.VMEM((TICKS - 1, NH, BT, 256), BF16),
            pltpu.VMEM((TICKS, NH, BT, 256), BF16),
            pltpu.VMEM((TICKS, blocks, BT, FD), BF16),
            pltpu.VMEM((3, 2, CD, D), BF16),
            pltpu.VMEM((NP, 128, 256), BF16),
            pltpu.VMEM((1, D), F32),
            pltpu.VMEM((TICKS, NH, BT, 256), BF16),
            pltpu.VMEM((NH, BT, 256), BF16),
            pltpu.VMEM((2, 3, 3, 1, CD), F32),
            pltpu.VMEM((2, CD, 128), F32),
            pltpu.VMEM((2, 1, CD), F32),
            pltpu.VMEM((8, 384), F32),
            pltpu.VMEM((128, 128), F32),
            pltpu.VMEM((TICKS, NH, 8 + BT, 384), F32),
            pltpu.VMEM((TICKS, BT + SEQ, 128), F32),
            dma((1,)),
            dma((8,)),
            dma((8,)),
            dma((8,)),
            dma((TICKS, NH)),
            dma((TICKS, NH, NP)),
            dma((TICKS, NH)),
            dma((TICKS, NH, NP)),
            dma((TICKS, NH)),
            dma((TICKS, NH)),
            dma((TICKS, 4)),
            dma((TICKS, 4)),
            dma((TICKS, NH)),
            dma((TICKS, NH)),
            dma(()),
        ],
        compiler_params=pltpu.CompilerParams(
            collective_id=0, has_side_effects=True, vmem_limit_bytes=56 << 20
        ),
    )(fresh, waiting, norm_gain, w_in, taps, filter_taps, decay_rate, w_out3)
    return made.reshape(1, TICKS, SEQ, FD)


def solution(mesh):
    return jax.shard_map(
        body,
        mesh=mesh,
        in_specs=(
            P(None, None, "dp"),
            P("section", None, "dp"),
            P("section", None),
            P("section", None, "dp", None),
            P("section", None, "dp", None),
            P("section", "dp", None),
            P("section", "dp"),
            P("section", None, "dp"),
        ),
        out_specs=P("section", None, None, "dp"),
        check_vma=False,
    )
```

time: 633 us -> 98 us (0.15)
  waiting for transfers between devices: 564 us -> 0 us
  Pallas kernels: 0 us -> 96.3 us
  matrix products: 31.2 us -> 0 us
  between operations: 13.7 us -> 0.01 us
  other arithmetic: 8.37 us -> 0 us
  local copies, waits for them, and re-layouts: 8.34 us -> 1.54 us
  starting transfers between devices: 6.59 us -> 0 us
    all_gather x6 -> x0, waiting for transfers between devices: 470 us -> none  [the longest x3 245 us: body(): lax.all_gather(y_local, 'dp', axis=1, tiled=True)]
    pallas_call x0 -> x1, Pallas kernels: none -> 96.3 us  [body(): pl.pallas_call(kernel, name='relay', out_shape=jax.ShapeDtypeStruct((TICK...]
    ppermute x2 -> x0, waiting for transfers between devices: 94.2 us -> none  [shifted(): return lax.ppermute(value, axis, pairs)]
    dot_general x10 -> x0, matrix products: 31.2 us -> none  [the longest x3 11 us: mixing(): jnp.einsum('cts,sc->tc', toeplitz, product, precision=lax.Precision.HIGHEST)]
    ppermute x2 -> x0, starting transfers between devices: 6.38 us -> none  [shifted(): return lax.ppermute(value, axis, pairs)]
  transfers between devices with their start and end apart: 8 -> 0, of which waited for: 8 -> 0; matrix products, arithmetic and copies ran while one was open for 2% -> 0% of each run, Pallas kernels for 0% -> 0%
where the time goes in v3:
time: 98 us; the launch traced here: 97.9 us
  Pallas kernels  96.3 us (98%)
  local copies, waits for them, and re-layouts  1.54 us (2%)
    pallas_call x1, Pallas kernels, body(): pl.pallas_call(kernel, name='relay', out_shape=jax.ShapeDtypeStruct((TICK...  96.3 us

profile of v3, /device:TPU:1, one launch (start us, length us, event | category | flops | bytes accessed | tf_op | source)
XLA Modules:
  0.0 97.9 jit_solution(6995466147090874530)
XLA Ops:
  0.0 96.3 %relay.1 = bf16[3,4,32,128]{3,2,1,0:T(8,128)(2,1)} custom-call(bf16[3,4,32,128]{3,2,1,0:T(8,128)(2,1)} %bitcast.7, bf16[4,32,128]{2,1,0:T(8,128)(2,1)} %bitcast.8, f32[1,8192]{1,0:T(1,128)} %gain.1, bf16[1,3,64,8192]{3,2,1,0:T(8,128)(2,1)} %w_in.1, f32[3,3,1,64]{3,2,1,0:T(1,128)} %bitcast.9, f32[1,64,128]{2,1,0:T(8,128)} %long_hbm.1, f32[1,64]{1,0:T(1,128)} %decay_hbm.1, ...), custom_call_target="tpu_custom_call" | custom-call | tf_op jit(solution)/shard_map/relay/pallas_call | solution.py:312
  96.3 1.5 %copy.10 = bf16[1,3,128,128]{3,2,1,0:T(8,128)(2,1)} copy(bf16[1,3,128,128]{3,2,1,0:T(8,128)(2,1)} %bitcast.6) | data formatting | bytes 196608

commit v4 on v3

--- a/solution.py
+++ b/solution.py
@@ -257,11 +257,16 @@
         block = 2 * h + c
         result[k, block] = jnp.where(c == 0, final[:, 0:128], final[:, 128:256])
         out_copy(k, h).start()
+        own_copy(k, h).start()
+
+    def own_copy(k, h):
+        block = 2 * h + c
+        return local(result.at[k, block], out.at[k, block], sem_out.at[k, h])
 
     def out_copy(k, h):
         block = 2 * h + c
         return remote(
-            final_v.at[k, h, :, other], result.at[k, block], o_send.at[k, h], o_recv.at[k, h], sibling
+            final_v.at[k, h, :, other], out.at[k, block], o_send.at[k, h], o_recv.at[k, h], sibling
         )
 
     for k in range(TICKS):
@@ -277,11 +282,6 @@
         combine(k, 0)
         combine(k, 1)
 
-    for k in range(TICKS):
-        for h in range(NH):
-            out_copy(k, h).wait_recv()
-    put = local(result, out, sem_out)
-    put.start()
     for src, dst, n in pairs:
         remote(src, dst, sem_xsend.at[n], sem_xrecv.at[n], sibling).wait_send()
     half_wait(sem_xsend.at[0], carried_v.at[:, :, other])
@@ -289,7 +289,8 @@
     half_wait(sem_xsend.at[7], fresh_v.at[later, :, :, other])
     for k in range(TICKS):
         for h in range(NH):
-            out_copy(k, h).wait_send()
+            out_copy(k, h).wait()
+            own_copy(k, h).wait()
             drain(acts.at[k, h], a_send.at[k, h], NP if k else NP - 1)
             drain(gated.at[k, h], y_send.at[k, h], NP - 1)
             for cc in range(2):
@@ -298,7 +299,6 @@
                     def _():
                         tail_copy(k, h, cc).wait_send()
                         history_copy(k, 2 * h + cc).wait_send()
-    put.wait()
 
 
 def body(fresh_acts, carried, norm_gain, w_in, short_filter, filter_taps, decay_rate, w_out):
@@ -347,7 +347,7 @@
             dma((TICKS, 4)),
             dma((TICKS, NH)),
             dma((TICKS, NH)),
-            dma(()),
+            dma((TICKS, NH)),
         ],
         compiler_params=pltpu.CompilerParams(
             collective_id=0, has_side_effects=True, vmem_limit_bytes=56 << 20

time: 98 us -> 97.6 us (level)
  no operation moved by 1% of the time
where the time goes in v4:
time: 97.6 us; the launch traced here: 97.4 us
  Pallas kernels  95.9 us (98%)
  local copies, waits for them, and re-layouts  1.54 us (2%)
    pallas_call x1, Pallas kernels, body(): pl.pallas_call(kernel, name='relay', out_shape=jax.ShapeDtypeStruct((TICK...  95.9 us

profile of v4, /device:TPU:1, one launch (start us, length us, event | category | flops | bytes accessed | tf_op | source)
XLA Modules:
  0.0 97.4 jit_solution(5575056911108264178)
XLA Ops:
  0.0 95.9 %relay.1 = bf16[3,4,32,128]{3,2,1,0:T(8,128)(2,1)} custom-call(bf16[3,4,32,128]{3,2,1,0:T(8,128)(2,1)} %bitcast.7, bf16[4,32,128]{2,1,0:T(8,128)(2,1)} %bitcast.8, f32[1,8192]{1,0:T(1,128)} %gain.1, bf16[1,3,64,8192]{3,2,1,0:T(8,128)(2,1)} %w_in.1, f32[3,3,1,64]{3,2,1,0:T(1,128)} %bitcast.9, f32[1,64,128]{2,1,0:T(8,128)} %long_hbm.1, f32[1,64]{1,0:T(1,128)} %decay_hbm.1, ...), custom_call_target="tpu_custom_call" | custom-call | tf_op jit(solution)/shard_map/relay/pallas_call | solution.py:312
  95.9 1.5 %copy.10 = bf16[1,3,128,128]{3,2,1,0:T(8,128)(2,1)} copy(bf16[1,3,128,128]{3,2,1,0:T(8,128)(2,1)} %bitcast.6) | data formatting | bytes 196608
